TPU v7x, 128 devices: a whole 4x4x4 slice. The times are simulated.
128 devices in a mesh: seq: 16 (over x_hi, y, core), fsdp: 2 (over x_lo), dp: 4 (over z).
Axes of the slice: x: 4 (x_hi: 2, x_lo: 2; x = x_hi * 2 + x_lo), y: 4, z: 4, core: 2. Of those that a mesh axis runs over, the one named last changes fastest.
Arguments:
- queries: bfloat16 [8, 4096, 4096], P(('fsdp', 'dp'), 'seq'), may hold values from -160 to 160
- hidden: bfloat16 [8, 4096, 8192], P(('fsdp', 'dp'), 'seq'), may hold values from -8 to 8
- key_weight: bfloat16 [8192, 512], P('fsdp'), may hold values from -1 to 1
- doc_lengths: int32 [8, 32], P(('fsdp', 'dp')), may hold values from 1 to 256, 4096 in all within a row
- entropy_cot: bfloat16 [8, 4096, 32], P(('fsdp', 'dp'), 'seq'), may hold values from -600 to 600
Outputs:
- entropy: float32 [8, 4096, 32], P(('fsdp', 'dp'), 'seq')
- grad_queries: bfloat16 [8, 4096, 4096], P(('fsdp', 'dp'), 'seq')
- grad_key_weight: bfloat16 [8192, 512], P('fsdp')
Inputs may be any that keep to these rules, and one draw needn't show every extreme that they name: `doc_lengths`: each sequence's 32 documents are packed in order, their lengths sum to 4096, and the longest is exactly 256.
All inputs are finite; a program needn't handle non-finite values.
Results may differ from a plain program's by a relative error of at most 0.0088.
Values may be sent and summed in bfloat16 or wider, within the bound.
No kernel may reach another device: no remote copies, remote signals or barrier semaphores. Data moves between devices by JAX's collectives and lax.ppermute only.
A program may use at most 128 MiB of HBM per device.

v0:
```python
import jax
import jax.numpy as jnp
from jax import lax
from jax.sharding import PartitionSpec as P

QH = 32
KVH = 4
HD = 128


def document_index(lengths, seq_len):
    ends = jnp.cumsum(lengths)
    position = jnp.arange(seq_len, dtype=jnp.int32)
    return jnp.sum((ends[None, :] <= position[:, None]).astype(jnp.int32), axis=1)


def attend(queries, key_rows, cotangent, doc_index, doc_len):
    row_count, key_heads, group_size, head_size = queries.shape
    full_len = key_rows.shape[0]
    block_rows = min(512, row_count)
    window = block_rows + doc_len
    factor = head_size ** (-0.5)
    keys_padded = jnp.concatenate(
        [jnp.zeros((doc_len, key_heads, head_size), key_rows.dtype), key_rows], axis=0
    )
    index_padded = jnp.concatenate([jnp.full((doc_len,), -1, jnp.int32), doc_index], axis=0)

    def one_block(step_index, state_now):
        entropy, grad_query, grad_key = state_now
        row_start = (step_index * block_rows).astype(jnp.int32)
        query_block = lax.dynamic_slice_in_dim(queries, row_start, block_rows, 0)
        weight_block = lax.dynamic_slice_in_dim(cotangent, row_start, block_rows, 0).astype(
            jnp.float32
        )
        key_block = lax.dynamic_slice_in_dim(keys_padded, row_start, window, 0)
        key_docs = lax.dynamic_slice_in_dim(index_padded, row_start, window, 0)
        query_docs = lax.dynamic_slice_in_dim(doc_index, row_start, block_rows, 0)
        query_pos = row_start + jnp.arange(block_rows, dtype=jnp.int32)
        key_pos = row_start - doc_len + jnp.arange(window, dtype=jnp.int32)
        visible = (query_docs[:, None] == key_docs[None, :]) & (
            key_pos[None, :] <= query_pos[:, None]
        )
        scores = (
            jnp.einsum("rkgd,wkd->kgrw", query_block, key_block, preferred_element_type=jnp.float32)
            * factor
        )
        scores = jnp.where(visible, scores, -1e30)
        row_max = jnp.max(scores, axis=-1, keepdims=True)
        powers = jnp.exp(scores - row_max)
        denominator = jnp.sum(powers, axis=-1, keepdims=True)
        probability = powers / denominator
        mean_score = jnp.sum(jnp.where(visible, probability * scores, 0.0), axis=-1, keepdims=True)
        block_entropy = (row_max + jnp.log(denominator) - mean_score)[..., 0]
        row_weight = jnp.transpose(weight_block, (1, 2, 0))[..., None]
        slope = jnp.where(visible, row_weight * probability * (mean_score - scores), 0.0).astype(
            jnp.bfloat16
        )
        query_part = (
            jnp.einsum("kgrw,wkd->rkgd", slope, key_block, preferred_element_type=jnp.float32)
            * factor
        )
        key_part = (
            jnp.einsum("kgrw,rkgd->wkd", slope, query_block, preferred_element_type=jnp.float32)
            * factor
        )
        entropy = lax.dynamic_update_slice_in_dim(
            entropy, jnp.transpose(block_entropy, (2, 0, 1)), row_start, 0
        )
        grad_query = lax.dynamic_update_slice_in_dim(grad_query, query_part, row_start, 0)
        previous = lax.dynamic_slice_in_dim(grad_key, row_start, window, 0)
        grad_key = lax.dynamic_update_slice_in_dim(grad_key, previous + key_part, row_start, 0)
        return (entropy, grad_query, grad_key)

    initial = (
        jnp.zeros((row_count, key_heads, group_size), jnp.float32),
        jnp.zeros((row_count, key_heads, group_size, head_size), jnp.float32),
        jnp.zeros((full_len + doc_len, key_heads, head_size), jnp.float32),
    )
    entropy, grad_query, grad_key = lax.fori_loop(0, row_count // block_rows, one_block, initial)
    return (entropy, grad_query, grad_key[doc_len:])


def shards(queries, hidden, key_weight, doc_lengths, entropy_cot):
    tokens = hidden[0]
    local_rows = tokens.shape[0]
    seq_parts = lax.axis_size("seq")
    seq_len = local_rows * seq_parts
    group_size = QH // KVH
    doc_index = document_index(doc_lengths[0], seq_len)
    columns = tokens
    key_local = jnp.dot(
        columns,
        lax.all_gather(key_weight, "fsdp", axis=0, tiled=True),
        preferred_element_type=jnp.float32,
    ).astype(jnp.bfloat16)
    query_local = queries[0]
    cot_local = entropy_cot[0]
    share = QH // seq_parts
    outgoing = jnp.broadcast_to(
        key_local.reshape(local_rows, KVH, 1, HD), (local_rows, KVH, group_size, HD)
    )
    outgoing = outgoing.reshape(local_rows, KVH * group_size * HD)
    query_heads, key_heads_seq, cot_heads = (
        lax.all_to_all(query_local, "seq", split_axis=1, concat_axis=0, tiled=True),
        lax.all_to_all(outgoing, "seq", split_axis=1, concat_axis=0, tiled=True),
        lax.all_to_all(cot_local, "seq", split_axis=1, concat_axis=0, tiled=True),
    )
    key_count = key_heads_seq.shape[1] // HD
    entropy, grad_query, grad_key = attend(
        query_heads.reshape(seq_len, key_count, share // key_count, HD),
        key_heads_seq.reshape(seq_len, key_count, HD),
        cot_heads.reshape(seq_len, key_count, share // key_count),
        doc_index,
        local_rows,
    )
    grad_local, key_grad_local, entropy_local = (
        lax.all_to_all(
            grad_query.reshape(seq_len, share * HD), "seq", split_axis=0, concat_axis=1, tiled=True
        ),
        lax.all_to_all(
            grad_key.reshape(seq_len, key_count * HD),
            "seq",
            split_axis=0,
            concat_axis=1,
            tiled=True,
        ),
        lax.all_to_all(
            entropy.reshape(seq_len, share), "seq", split_axis=0, concat_axis=1, tiled=True
        ),
    )
    key_grad = jnp.sum(key_grad_local.reshape(local_rows, KVH, -1, HD), axis=2).reshape(
        local_rows, KVH * HD
    )
    key_grad_low = key_grad.astype(jnp.bfloat16)
    columns = tokens
    term_rows = lax.psum_scatter(
        lax.dot_general(
            columns, key_grad_low, (((0,), (0,)), ((), ())), preferred_element_type=jnp.float32
        ),
        "fsdp",
        scatter_dimension=0,
        tiled=True,
    )
    summed = lax.psum(term_rows, ("seq", "dp"))
    norm_factor = (seq_len * lax.axis_size("fsdp") * lax.axis_size("dp")) ** (-0.5)
    weight_grad = (summed * norm_factor).astype(jnp.bfloat16)
    return (
        entropy_local.reshape(1, local_rows, QH),
        grad_local.astype(jnp.bfloat16).reshape(1, local_rows, QH * HD),
        weight_grad,
    )


def solution(mesh):
    return jax.shard_map(
        shards,
        mesh=mesh,
        in_specs=(
            P(("fsdp", "dp"), "seq", None),
            P(("fsdp", "dp"), "seq", None),
            P("fsdp", None),
            P(("fsdp", "dp"), None),
            P(("fsdp", "dp"), "seq", None),
        ),
        out_specs=(P(("fsdp", "dp"), "seq", None), P(("fsdp", "dp"), "seq", None), P("fsdp", None)),
        check_vma=False,
    )
```

profile of v0, /device:TPU:0, one launch (start us, length us, event | category | flops | bytes accessed | tf_op | source)
XLA Modules:
  0.0 1256.6 jit_solution(18081824443787886025)
XLA Ops:
  11.2 7.1 all-to-all-start.1
  18.3 114.7 %all-gather.2.cloned.1.call-done = bf16[8192,512]{1,0:T(8,128)(2,1)} async-done(((bf16[4096,512]{1,0:T(8,128)(2,1)}), bf16[8192,512]{1,0:T(8,128)(2,1)}) %all-gather.2.cloned.1.call-update) | async-done | bytes 8388624 | tf_op jit(solution)/shard_map/all_gather | solution.py:93
  133.0 7.0 fusion.41
  141.7 8.3 all-to-all-start
  150.9 28.5 %all-to-all-done = bf16[256,16,256]{0,2,1:T(8,128)(2,1)} async-done(((bf16[256,16,256]{0,2,1:T(8,128)(2,1)}), bf16[256,16,256]{0,2,1:T(8,128)(2,1)}, u32[]{:S(2)}, u32[]{:S(2)}) %all-to-all-start) | async-done | bytes 2097184 | tf_op jit(solution)/shard_map/all_to_all | solution.py:105
  179.3 6.3 all-to-all-start.2
  188.5 4.2 reshape.222
  192.7 4.1 copy.82
  204.4 88.0 %while.19 = (s32[]{:T(128)}, f32[4096,2,1]{0,1,2:T(2,128)}, bf16[4096,2,1,128]{0,3,1,2:T(8,128)(2,1)S(1)}, f32[4352,2,128]{0,2,1:T(8,128)}, s32[4096]{0:T(1024)S...) while((s32[]{:T(128)}, f32[4096,2,1]{0,1,2:T(2,128)}, ...), condition=%wide.region_6.7_spmd, body=%wide.region_2.6_spmd.sunk | while | flops 630850816 | bytes 21601552 | solution.py:79
  244.7 3.7 fusion.61
  255.7 3.7 fusion.61
  277.7 3.7 fusion.61
  288.7 3.7 fusion.61
  299.1 58.8 %all_to_all.93 = f32[16,256,256]{1,2,0:T(8,128)} all-to-all(f32[16,256,256]{1,2,0:T(8,128)S(1)} %copy.90), channel_id=1, replica_groups=mesh['seq'=16,'fsdp'=2,'dp'=4] {'seq'}, dimensions={0} | all-to-all | bytes 8388608 | tf_op jit(solution)/shard_map/all_to_all | solution.py:120
  360.4 10.3 convolution_bitcast_fusion
  370.7 189.8 %reduce-scatter.2.cloned.1.call-done = f32[4096,512]{0,1:T(8,128)} async-done(((f32[8192,512]{0,1:T(8,128)}), f32[4096,512]{0,1:T(8,128)}) %reduce-scatter.2.cloned.1.call-update) | async-done | bytes 8388624 | tf_op jit(solution)/shard_map/reduce_scatter | solution.py:136
  560.6 6.5 all-to-all-start.3
  569.1 4.3 copy.98
  574.7 5.9 all-to-all-start.4
  581.2 29.5 %all-to-all-done.4 = bf16[16,256,256]{2,1,0:T(8,128)(2,1)S(1)} async-done(((bf16[16,256,256]{2,1,0:T(8,128)(2,1)}), bf16[16,256,256]{2,1,0:T(8,128)(2,1)S(1)}, u32[]{:S(2)}, u32[]{:S(2)}) %all-to-all-start.4) | async-done | bytes 2097184 | tf_op jit(solution)/shard_map/all_to_all | solution.py:117
  613.0 4.1 copy.91
  617.1 620.1 %all-reduce.4.cloned.1.call-done = f32[4096,512]{0,1:T(8,128)} async-done(((f32[4096,512]{0,1:T(8,128)}), f32[4096,512]{0,1:T(8,128)}) %all-reduce.4.cloned.1.call-update) | async-done | bytes 8388624 | tf_op jit(solution)/shard_map/psum | solution.py:144
  1237.3 6.4 multiply_convert_fusion
  1243.6 6.4 copy.92
  (129 shorter events, 105.7 us)
Async XLA Ops:
  7.2 1.6 copy-start
  7.2 125.8 %all-gather.2.cloned.1.call-start = ((), (), s32[]{:S(2)}) async-start(), calls=%async_computation.7 | async-start | bytes 12582912 | tf_op jit(solution)/shard_map/all_gather | solution.py:93
  11.2 128.9 %all-to-all-start.1 = ((bf16[256,16,256]{0,2,1:T(8,128)(2,1)}), bf16[256,16,256]{0,2,1:T(8,128)(2,1)S(1)}, u32[]{:S(2)}, u32[]{:S(2)}) async-start(bf16[256,16,256]{0,2,1:T(8,128)(2,1)} %bitcast.144), calls=%async_computation.1 | async-start | bytes 4194304 | tf_op jit(solution)/shard_map/all_to_all | solution.py:104
  140.1 9.9 copy-start.2
  140.1 10.1 copy-start.1
  141.7 37.6 %all-to-all-start = ((bf16[256,16,256]{0,2,1:T(8,128)(2,1)}), bf16[256,16,256]{0,2,1:T(8,128)(2,1)}, u32[]{:S(2)}, u32[]{:S(2)}) async-start(bf16[256,16,256]{0,2,1:T(8,128)(2,1)} %bitcast.145), calls=%async_computation | async-start | bytes 4194304 | tf_op jit(solution)/shard_map/all_to_all | solution.py:105
  179.3 21.9 %all-to-all-start.2 = ((bf16[256,16,2]{0,2,1:T(2,128)(2,1)}), bf16[256,16,2]{0,2,1:T(2,128)(2,1)S(1)}, u32[]{:S(2)}, u32[]{:S(2)}) async-start(bf16[256,16,2]{0,2,1:T(2,128)(2,1)} %all_to_all.76), calls=%async_computation.2 | async-start | bytes 32768 | tf_op jit(solution)/shard_map/all_to_all | solution.py:106
  185.6 374.9 %reduce-scatter.2.cloned.1.call-start = ((), (), s32[]{:S(2)}) async-start(), calls=%async_computation.8 | async-start | bytes 25165824 | tf_op jit(solution)/shard_map/reduce_scatter | solution.py:136
  370.7 866.6 %all-reduce.4.cloned.1.call-start = ((), (), s32[]{:S(2)}) async-start(), calls=%async_computation.9 | async-start | bytes 16777216 | tf_op jit(solution)/shard_map/psum | solution.py:144
  560.6 14.1 %all-to-all-start.3 = ((f32[16,256,2]{1,2,0:T(2,128)}), f32[16,256,2]{1,2,0:T(2,128)S(1)}, u32[]{:S(2)}, u32[]{:S(2)}) async-start(f32[16,256,2]{1,2,0:T(2,128)} %bitcast.20), calls=%async_computation.3 | async-start | bytes 65536 | tf_op jit(solution)/shard_map/all_to_all | solution.py:127
  574.7 36.0 %all-to-all-start.4 = ((bf16[16,256,256]{2,1,0:T(8,128)(2,1)}), bf16[16,256,256]{2,1,0:T(8,128)(2,1)S(1)}, u32[]{:S(2)}, u32[]{:S(2)}) async-start(bf16[16,256,256]{2,1,0:T(8,128)(2,1)} %copy.98), calls=%async_computation.4 | async-start | bytes 4194304 | tf_op jit(solution)/shard_map/all_to_all | solution.py:117
Sparse Core Ops, SparseCore 0:
  9.7 123.2 all-gather.1
  370.8 189.6 reduce-scatter.1
  563.2 674.0 all-reduce.3
where the time goes:
time: 1260 us
  waiting for transfers between devices  985 us (78%)
  matrix products  81.7 us (6%)
  blocking collectives  58.8 us (5%)
  local copies, waits for them, and re-layouts  51.6 us (4%)
  starting transfers between devices  34.4 us (3%)
  other arithmetic  31.4 us (2%)
  between operations  13.9 us (1%)
    psum x1, waiting for transfers between devices, shards(): summed = lax.psum(term_rows, ('seq', 'dp'))  620 us
    reduce_scatter x1, waiting for transfers between devices, shards(): lax.psum_scatter(lax.dot_general(columns, key_grad_low, (((0,), (0,)), ((...  190 us
    all_gather x1, waiting for transfers between devices, shards(): lax.all_gather(key_weight, 'fsdp', axis=0, tiled=True)  115 us
    all_to_all x1, blocking collectives, shards(): lax.all_to_all(grad_key.reshape(seq_len, key_count * HD), 'seq', split_ax...  58.8 us
    all_to_all x1, waiting for transfers between devices, shards(): lax.all_to_all(grad_query.reshape(seq_len, share * HD), 'seq', split_axis...  29.5 us
    dot_general x8, matrix products, one_block(): jnp.einsum('kgrw,rkgd->wkd', slope, query_block, preferred_element_type=j...  29.3 us
    all_to_all x1, waiting for transfers between devices, shards(): lax.all_to_all(outgoing, 'seq', split_axis=1, concat_axis=0, tiled=True)  28.5 us
  transfers between devices with their start and end apart: 8, of which 6 were waited for; matrix products, arithmetic and copies ran while one was open for 3% of the time, Pallas kernels for 0%

commit v1 on v0

--- a/solution.py
+++ b/solution.py
@@ -6,6 +6,10 @@
 QH = 32
 KVH = 4
 HD = 128
+
+
+def carry_leaves_for(body):
+    return lax.psum(lax.psum(body, axis_name="dp"), axis_name="seq")
 
 
 def document_index(lengths, seq_len):
@@ -141,7 +145,7 @@
         scatter_dimension=0,
         tiled=True,
     )
-    summed = lax.psum(term_rows, ("seq", "dp"))
+    summed = carry_leaves_for(term_rows)
     norm_factor = (seq_len * lax.axis_size("fsdp") * lax.axis_size("dp")) ** (-0.5)
     weight_grad = (summed * norm_factor).astype(jnp.bfloat16)
     return (

time: 1260 us -> 930 us (0.74)
  waiting for transfers between devices: 985 us -> 656 us
    psum x1 -> x2, waiting for transfers between devices: 620 us -> 280 us  [carry_leaves_for(): return lax.psum(lax.psum(body, axis_name='dp'), axis_name='seq')]
  transfers between devices with their start and end apart: 8 -> 9, of which waited for: 6 -> 7; matrix products, arithmetic and copies ran while one was open for 3% -> 4% of each run, Pallas kernels for 0% -> 0%
where the time goes in v1:
time: 930 us; the launch traced here: 928 us
  waiting for transfers between devices  656 us (71%)
  matrix products  81.7 us (9%)
  blocking collectives  58.8 us (6%)
  local copies, waits for them, and re-layouts  51.6 us (6%)
  starting transfers between devices  34.6 us (4%)
  other arithmetic  31.3 us (3%)
  between operations  13.9 us (1%)
    psum x2, waiting for transfers between devices, carry_leaves_for(): return lax.psum(lax.psum(body, axis_name='dp'), axis_name='seq')  280 us
    reduce_scatter x1, waiting for transfers between devices, shards(): lax.psum_scatter(lax.dot_general(columns, key_grad_low, (((0,), (0,)), ((...  190 us
    all_gather x1, waiting for transfers between devices, shards(): lax.all_gather(key_weight, 'fsdp', axis=0, tiled=True)  115 us
    all_to_all x1, blocking collectives, shards(): lax.all_to_all(grad_key.reshape(seq_len, key_count * HD), 'seq', split_ax...  58.8 us
    all_to_all x1, waiting for transfers between devices, shards(): lax.all_to_all(grad_query.reshape(seq_len, share * HD), 'seq', split_axis...  41.5 us
    dot_general x8, matrix products, one_block(): jnp.einsum('kgrw,rkgd->wkd', slope, query_block, preferred_element_type=j...  29.3 us
    all_to_all x1, waiting for transfers between devices, shards(): lax.all_to_all(outgoing, 'seq', split_axis=1, concat_axis=0, tiled=True)  28.5 us
    dot_general x8, matrix products, one_block(): jnp.einsum('kgrw,wkd->rkgd', slope, key_block, preferred_element_type=jnp...  19.7 us
  transfers between devices with their start and end apart: 9, of which 7 were waited for; matrix products, arithmetic and copies ran while one was open for 4% of the time, Pallas kernels for 0%

profile of v1, /device:TPU:0, one launch (start us, length us, event | category | flops | bytes accessed | tf_op | source)
XLA Modules:
  0.0 928.4 jit_solution(15943684415915102141)
XLA Ops:
  11.2 7.1 all-to-all-start.1
  18.3 114.7 %all-gather.2.cloned.1.call-done = bf16[8192,512]{1,0:T(8,128)(2,1)} async-done(((bf16[4096,512]{1,0:T(8,128)(2,1)}), bf16[8192,512]{1,0:T(8,128)(2,1)}) %all-gather.2.cloned.1.call-update) | async-done | bytes 8388624 | tf_op jit(solution)/shard_map/all_gather | solution.py:97
  133.0 7.0 fusion.41
  141.7 8.3 all-to-all-start
  150.9 28.5 %all-to-all-done = bf16[256,16,256]{0,2,1:T(8,128)(2,1)} async-done(((bf16[256,16,256]{0,2,1:T(8,128)(2,1)}), bf16[256,16,256]{0,2,1:T(8,128)(2,1)}, u32[]{:S(2)}, u32[]{:S(2)}) %all-to-all-start) | async-done | bytes 2097184 | tf_op jit(solution)/shard_map/all_to_all | solution.py:109
  179.3 6.3 all-to-all-start.2
  188.5 4.2 reshape.222
  192.7 4.1 copy.82
  204.4 88.0 %while.19 = (s32[]{:T(128)}, f32[4096,2,1]{0,1,2:T(2,128)}, bf16[4096,2,1,128]{0,3,1,2:T(8,128)(2,1)S(1)}, f32[4352,2,128]{0,2,1:T(8,128)}, s32[4096]{0:T(1024)S...) while((s32[]{:T(128)}, f32[4096,2,1]{0,1,2:T(2,128)}, ...), condition=%wide.region_6.7_spmd, body=%wide.region_2.6_spmd.sunk | while | flops 630850816 | bytes 21601552 | solution.py:83
  255.7 3.7 fusion.61
  277.7 3.7 fusion.61
  288.7 3.7 fusion.61
  299.1 58.8 %all_to_all.93 = f32[16,256,256]{1,2,0:T(8,128)} all-to-all(f32[16,256,256]{1,2,0:T(8,128)S(1)} %copy.90), channel_id=1, replica_groups=mesh['seq'=16,'fsdp'=2,'dp'=4] {'seq'}, dimensions={0} | all-to-all | bytes 8388608 | tf_op jit(solution)/shard_map/all_to_all | solution.py:124
  360.4 10.3 %convolution_bitcast_fusion = f32[8192,512]{0,1:T(8,128)} fusion(bf16[256,512]{0,1:T(8,128)(2,1)S(1)} %bitcast.150, bf16[1,256,8192]{2,1,0:T(8,128)(2,1)} %param.8), kind=kOutput, calls=%fused_computation.33 | convolution fusion | flops 2147483648 | bytes 21233664 | tf_op jit(solution)/shard_map/dot_general | solution.py:141
  370.7 189.8 %reduce-scatter.2.cloned.1.call-done = f32[4096,512]{0,1:T(8,128)} async-done(((f32[8192,512]{0,1:T(8,128)}), f32[4096,512]{0,1:T(8,128)}) %reduce-scatter.2.cloned.1.call-update) | async-done | bytes 8388624 | tf_op jit(solution)/shard_map/reduce_scatter | solution.py:140
  560.6 164.0 %all-reduce.5.cloned.1.call-done = f32[4096,512]{0,1:T(8,128)} async-done(((f32[4096,512]{0,1:T(8,128)}), f32[4096,512]{0,1:T(8,128)}) %all-reduce.5.cloned.1.call-update) | async-done | bytes 8388624 | tf_op jit(solution)/shard_map/psum | solution.py:12
  724.7 6.8 all-to-all-start.3
  733.5 4.3 copy.98
  739.2 5.8 all-to-all-start.4
  745.6 41.5 %all-to-all-done.4 = bf16[16,256,256]{2,1,0:T(8,128)(2,1)S(1)} async-done(((bf16[16,256,256]{2,1,0:T(8,128)(2,1)}), bf16[16,256,256]{2,1,0:T(8,128)(2,1)S(1)}, u32[]{:S(2)}, u32[]{:S(2)}) %all-to-all-start.4) | async-done | bytes 2097184 | tf_op jit(solution)/shard_map/all_to_all | solution.py:121
  789.5 4.1 copy.91
  793.6 115.6 %all-reduce.7.cloned.1.call-done = f32[4096,512]{0,1:T(8,128)} async-done(((f32[4096,512]{0,1:T(8,128)}), f32[4096,512]{0,1:T(8,128)}) %all-reduce.7.cloned.1.call-update) | async-done | bytes 8388624 | tf_op jit(solution)/shard_map/psum | solution.py:12
  909.2 6.3 multiply_convert_fusion
  915.5 6.4 copy.92
  (132 shorter events, 109.5 us)
Async XLA Ops:
  7.2 1.6 copy-start
  7.2 125.8 %all-gather.2.cloned.1.call-start = ((), (), s32[]{:S(2)}) async-start(), calls=%async_computation.7 | async-start | bytes 12582912 | tf_op jit(solution)/shard_map/all_gather | solution.py:97
  11.2 128.9 %all-to-all-start.1 = ((bf16[256,16,256]{0,2,1:T(8,128)(2,1)}), bf16[256,16,256]{0,2,1:T(8,128)(2,1)S(1)}, u32[]{:S(2)}, u32[]{:S(2)}) async-start(bf16[256,16,256]{0,2,1:T(8,128)(2,1)} %bitcast.144), calls=%async_computation.1 | async-start | bytes 4194304 | tf_op jit(solution)/shard_map/all_to_all | solution.py:108
  140.1 9.9 %copy-start.2 = (s32[1,32]{1,0:T(1,128)S(1)}, s32[1,32]{1,0:T(1,128)}, u32[]{:S(2)}) copy-start(s32[1,32]{1,0:T(1,128)} %param.10) | copy-start | bytes 388
  140.1 10.1 %copy-start.1 = (bf16[1,256,32]{1,2,0:T(8,128)(2,1)S(1)}, bf16[1,256,32]{1,2,0:T(8,128)(2,1)}, u32[]{:S(2)}) copy-start(bf16[1,256,32]{1,2,0:T(8,128)(2,1)} %param.11) | copy-start | bytes 49156
  141.7 37.6 %all-to-all-start = ((bf16[256,16,256]{0,2,1:T(8,128)(2,1)}), bf16[256,16,256]{0,2,1:T(8,128)(2,1)}, u32[]{:S(2)}, u32[]{:S(2)}) async-start(bf16[256,16,256]{0,2,1:T(8,128)(2,1)} %bitcast.145), calls=%async_computation | async-start | bytes 4194304 | tf_op jit(solution)/shard_map/all_to_all | solution.py:109
  179.3 21.9 %all-to-all-start.2 = ((bf16[256,16,2]{0,2,1:T(2,128)(2,1)}), bf16[256,16,2]{0,2,1:T(2,128)(2,1)S(1)}, u32[]{:S(2)}, u32[]{:S(2)}) async-start(bf16[256,16,2]{0,2,1:T(2,128)(2,1)} %all_to_all.76), calls=%async_computation.2 | async-start | bytes 32768 | tf_op jit(solution)/shard_map/all_to_all | solution.py:110
  185.6 374.9 %reduce-scatter.2.cloned.1.call-start = ((), (), s32[]{:S(2)}) async-start(), calls=%async_computation.8 | async-start | bytes 25165824 | tf_op jit(solution)/shard_map/reduce_scatter | solution.py:140
  370.7 354.0 %all-reduce.5.cloned.1.call-start = ((), (), s32[]{:S(2)}) async-start(), calls=%async_computation.9 | async-start | bytes 16777216 | tf_op jit(solution)/shard_map/psum | solution.py:12
  560.6 348.6 %all-reduce.7.cloned.1.call-start = ((), (), s32[]{:S(2)}) async-start(), calls=%async_computation.10 | async-start | bytes 16777216 | tf_op jit(solution)/shard_map/psum | solution.py:12
  724.7 14.5 %all-to-all-start.3 = ((f32[16,256,2]{1,2,0:T(2,128)}), f32[16,256,2]{1,2,0:T(2,128)S(1)}, u32[]{:S(2)}, u32[]{:S(2)}) async-start(f32[16,256,2]{1,2,0:T(2,128)} %bitcast.20), calls=%async_computation.3 | async-start | bytes 65536 | tf_op jit(solution)/shard_map/all_to_all | solution.py:131
  739.2 47.9 %all-to-all-start.4 = ((bf16[16,256,256]{2,1,0:T(8,128)(2,1)}), bf16[16,256,256]{2,1,0:T(8,128)(2,1)S(1)}, u32[]{:S(2)}, u32[]{:S(2)}) async-start(bf16[16,256,256]{2,1,0:T(8,128)(2,1)} %copy.98), calls=%async_computation.4 | async-start | bytes 4194304 | tf_op jit(solution)/shard_map/all_to_all | solution.py:121
Sparse Core Ops, SparseCore 0:
  9.7 123.2 all-gather.1
  370.8 189.6 reduce-scatter.1
  563.2 161.4 all-reduce.4
  727.2 181.9 all-reduce.6
